TPU v7x, 768 devices: a whole 4x8x12 slice. The times are simulated.
768 devices in a mesh: pb: 16 (over x, z_hi), ga: 48 (over z_lo, y, core).
Axes of the slice: x: 4, y: 8, z: 12 (z_hi: 4, z_lo: 3; z = z_hi * 3 + z_lo), core: 2. Of those that a mesh axis runs over, the one named last changes fastest.
Arguments:
- valence: bfloat16 [96, 16, 16, 4608], P('pb', None, None, 'ga'), may hold values from -6 to 6
- conduction: bfloat16 [96, 16, 8, 4608], P('pb', None, None, 'ga'), may hold values from -6 to 6
- screened: bfloat16 [16, 4608, 4608], P('pb', 'ga'), as said below
- kq_table: int32 [96, 16], P('pb'), may hold values from 0 to 15, each once within a row
Outputs:
- kernel: float32 [96, 16, 8, 16], P('pb')
Inputs may be any that keep to these rules, and one draw needn't show every extreme that they name: screened is symmetric in its last two dimensions: screened[q, G, H] = screened[q, H, G] exactly. Each row of kq_table names every label of 0 to 15 once.
All inputs are finite; a program needn't handle non-finite values.
Results may differ from a plain program's by a relative error of at most 0.0003.
Values may be sent and summed in bfloat16 or wider, within the bound.
A program may use at most 128 MiB of HBM per device.

v0:
```python
import jax
import jax.numpy as jnp
from jax import lax
from jax.sharding import PartitionSpec as P


def per_device(valence, conduction, screened, kq_table):
    valence_q, conduction_q = (
        lax.all_to_all(valence, "pb", split_axis=1, concat_axis=0, tiled=True),
        lax.all_to_all(conduction, "pb", split_axis=1, concat_axis=0, tiled=True),
    )
    applied = jnp.einsum(
        "qgh,kqph->qgkp",
        screened,
        lax.all_gather(valence_q, "ga", axis=3, tiled=True),
        preferred_element_type=jnp.float32,
    )
    partial_value = jnp.einsum(
        "kqcg,qgkv->kqcv",
        conduction_q.astype(jnp.float32),
        applied,
        precision=lax.Precision.HIGHEST,
    )
    summed = lax.psum(partial_value, "ga")
    returned = lax.all_to_all(summed, "pb", split_axis=0, concat_axis=1, tiled=True)
    q_total = returned.shape[1]
    labels = lax.iota(jnp.int32, q_total)
    onehot = (kq_table[:, :, None] == labels[None, None, :]).astype(jnp.float32)
    kernel = jnp.einsum("kqj,kqcv->kjcv", onehot, returned, precision=lax.Precision.HIGHEST)
    return kernel


def solution(mesh):
    return jax.shard_map(
        per_device,
        mesh=mesh,
        in_specs=(
            P("pb", None, None, "ga"),
            P("pb", None, None, "ga"),
            P("pb", "ga", None),
            P("pb", None),
        ),
        out_specs=P("pb", None, None, None),
        check_vma=False,
    )
```

profile of v0, /device:TPU:1, one launch (start us, length us, event | category | flops | bytes accessed | tf_op | source)
XLA Modules:
  0.0 549.0 jit_solution(6136320113983719711)
XLA Ops:
  6.5 0.0 copy-start
  6.5 0.0 all-gather.2.cloned.1.call-start
  6.5 1.1 copy.19
  7.6 31.9 %all_to_all.51 = bf16[6,16,16,96]{3,2,0,1:T(8,128)(2,1)S(1)} all-to-all(bf16[6,16,16,96]{3,2,0,1:T(8,128)(2,1)S(1)} %copy.19), channel_id=1, replica_groups=mesh['pb'=16,'ga'=48] {'pb'}, dimensions={1} | all-to-all | bytes 589824 | tf_op jit(solution)/shard_map/all_to_all | solution.py:9
  39.6 1.3 copy.20
  40.9 0.0 all-gather.2.cloned.1.call-update
  40.9 1.7 copy.22
  42.5 5.5 all-to-all-start.1
  48.0 204.3 %all-gather.2.cloned.1.call-done = bf16[96,1,16,4608]{0,2,1,3:T(8,128)(2,1)} async-done(((bf16[96,1,16,96]{0,2,1,3:T(8,128)(2,1)}), bf16[96,1,16,4608]{0,2,1,3:T(8,128)(2,1)}) %all-gather.2.cloned.1.call-update) | async-done | bytes 14155792 | tf_op jit(solution)/shard_map/all_gather | solution.py:15
  252.3 23.2 %copy.21 = bf16[96,1,16,4608]{3,0,2,1:T(8,128)(2,1)} copy(bf16[96,1,16,4608]{0,2,1,3:T(8,128)(2,1)} %all-gather.2.cloned.1.call-done) | data formatting | bytes 28311552 | tf_op jit(solution)/shard_map/all_gather | solution.py:15
  275.5 0.0 copy-done
  275.5 0.0 copy-start.1
  275.5 8.3 %fusion = f32[96,96,16]{1,0,2:T(8,128)S(1)} fusion(bf16[96,1,16,4608]{3,0,2,1:T(8,128)(2,1)} %copy.21, bf16[1,96,4608]{2,1,0:T(8,128)(2,1)S(1)} %copy-done), kind=kOutput, calls=%fused_computation | convolution fusion | flops 1358954496 | bytes 15630336 | tf_op jit(solution)/shard_map/qgh,kqph->qgkp/dot_general | solution.py:12
  283.9 0.4 copy.23
  284.3 0.0 all-to-all-done.1
  284.3 0.7 convolution_bitcast_fusion
  285.0 180.1 %psum.7 = f32[96,1,8,16]{3,2,0,1:T(8,128)S(1)} all-reduce(f32[96,1,8,16]{3,2,0,1:T(8,128)S(1)} %convolution_bitcast_fusion), channel_id=1, replica_groups=mesh['pb'=16,'ga'=48] {'ga'}, use_global_device_ids=true, to_apply=%region_0.0 | all-reduce | flops 12288 | bytes 98304 | tf_op jit(solution)/shard_map/psum | solution.py:24
  465.1 0.2 reshape.20
  465.3 74.1 %all_to_all.52 = f32[16,1,768]{2,1,0:T(1,128)S(1)} all-to-all(f32[16,1,768]{2,1,0:T(1,128)S(1)} %reshape.20), channel_id=1, replica_groups=mesh['pb'=16,'ga'=48] {'pb'}, dimensions={0} | all-to-all | bytes 98304 | tf_op jit(solution)/shard_map/all_to_all | solution.py:25
  539.4 0.5 broadcast.1
  539.9 0.8 reduce
  540.7 0.2 reshape.21
  540.9 0.0 copy-done.1
  540.9 0.4 fusion.3
  541.3 0.9 copy.26
Async XLA Ops:
  6.5 269.0 %copy-start = (bf16[1,96,4608]{2,1,0:T(8,128)(2,1)S(1)}, bf16[1,96,4608]{2,1,0:T(8,128)(2,1)}, u32[]{:S(2)}) copy-start(bf16[1,96,4608]{2,1,0:T(8,128)(2,1)} %param.6) | copy-start | bytes 2654212
  6.5 245.8 %all-gather.2.cloned.1.call-start = ((), (), s32[]{:S(2)}) async-start(), calls=%async_computation.3 | async-start | bytes 19267584 | tf_op jit(solution)/shard_map/all_gather | solution.py:15
  42.5 241.7 %all-to-all-start.1 = ((bf16[6,16,8,96]{3,2,0,1:T(8,128)(2,1)}), bf16[6,16,8,96]{3,2,0,1:T(8,128)(2,1)S(1)}, u32[]{:S(2)}, u32[]{:S(2)}) async-start(bf16[6,16,8,96]{3,2,0,1:T(8,128)(2,1)} %copy.22), calls=%async_computation.1 | async-start | bytes 393216 | tf_op jit(solution)/shard_map/all_to_all | solution.py:10
  275.5 265.3 %copy-start.1 = (s32[6,16]{1,0:T(8,128)S(1)}, s32[6,16]{1,0:T(8,128)}, u32[]{:S(2)}) copy-start(s32[6,16]{1,0:T(8,128)} %param.7) | copy-start | bytes 1156
Sparse Core Ops, SparseCore 0:
  41.0 211.2 all-gather.1
where the time goes:
time: 555 us; the launch traced here: 549 us
  blocking collectives  286 us (52%)
  waiting for transfers between devices  204 us (37%)
  local copies, waits for them, and re-layouts  29.4 us (5%)
  between operations  13.5 us (2%)
  matrix products  9.47 us (2%)
    all_gather x1, waiting for transfers between devices, per_device(): lax.all_gather(valence_q, 'ga', axis=3, tiled=True)  204 us
    psum x1, blocking collectives, per_device(): summed = lax.psum(partial_value, 'ga')  180 us
    all_to_all x1, blocking collectives, per_device(): lax.all_to_all(summed, 'pb', split_axis=0, concat_axis=1, tiled=True)  74.1 us
    all_to_all x1, blocking collectives, per_device(): lax.all_to_all(valence, 'pb', split_axis=1, concat_axis=0, tiled=True)  31.9 us
    all_gather x1, local copies, waits for them, and re-layouts, per_device(): lax.all_gather(valence_q, 'ga', axis=3, tiled=True)  23.2 us
  transfers between devices with their start and end apart: 2, of which 1 were waited for; matrix products, arithmetic and copies ran while one was open for 6% of the time, Pallas kernels for 0%

commit v1 on v0

v1 whole, which is shorter than its diff:
```python
import functools

import jax
import jax.numpy as jnp
from jax import lax
from jax.experimental import pallas as pl
from jax.experimental.pallas import tpu as pltpu
from jax.sharding import PartitionSpec as P

MESH = pl.DeviceIdType.MESH
X, ZH, ZL, Y, CORES = 4, 4, 3, 8, 2
NP, NJ = X * ZH, ZL * Y * CORES
ORDER = (0, 1, 3, 2)
REACH_UP = (4, 3, 3, 4)
REACH_DOWN = (3, 4, 4, 3)
SEQUENCE = tuple(
    item
    for place in range(len(ORDER) + 1)
    for item in (
        ([(ORDER[place], 0)] if place < len(ORDER) else [])
        + ([(ORDER[place - 1], z) for z in range(1, ZL)] if place else [])
    )
)


def kernel(
    val_ref, con_ref, w_ref, table_ref, out_ref,
    con_in, val_in, wide, right, wt, acc, part, tiles, total, back, label,
    con_sem, val_sem, hop_sem, pair_sem, tile_sem, back_sem, sent_sem,
):
    me_p, me_j = lax.axis_index("pb"), lax.axis_index("ga")
    x, zh = me_p // ZH, lax.rem(me_p, ZH)
    zl, y, core = me_j // (Y * CORES), lax.rem(me_j // CORES, Y), lax.rem(me_j, CORES)
    nk, _, npc, own = con_ref.shape
    npv = val_ref.shape[2]
    rows = nk * npc

    def p_of(px, pz):
        return px * ZH + lax.rem(pz, ZH)

    def j_of(jz, jy, jc):
        return (lax.rem(jz, ZL) * Y + lax.rem(jy, Y)) * CORES + jc

    def slot_of(sy, sc, sz, n):
        return ((lax.rem(sy, Y) * CORES + sc) * ZL + lax.rem(sz, ZL)) * ZH + n

    def send(src, dst, sent, arrived, p, j):
        pltpu.make_async_remote_copy(
            src_ref=src, dst_ref=dst, send_sem=sent, recv_sem=arrived, device_id=(p, j), device_id_type=MESH
        ).start()

    def wait(ref, sem):
        pltpu.make_async_copy(ref, ref, sem).wait()

    barrier = pltpu.get_barrier_semaphore()
    peers = [(p_of(lax.rem(x + dx, X), zh + dz), me_j) for dz in range(ZH) for dx in range(X) if dz or dx]
    peers += [(me_p, j_of(zl + d, y, core)) for d in range(1, ZL)]
    peers += [(me_p, j_of(zl, y + d, core)) for d in (1, Y - 1)] + [(me_p, j_of(zl, y, 1 - core))]
    for p, j in peers:
        pl.semaphore_signal(barrier, inc=1, device_id=(p, j), device_id_type=MESH)

    lane = lax.broadcasted_iota(jnp.int32, (npc, nk * npv), 1) // npv

    @pl.loop(0, w_ref.shape[2] // 128)
    def _(a):
        at = pl.multiple_of(a * 128, 128)
        block = w_ref[0, :, pl.ds(at, 128)].astype(jnp.float32)
        block = jnp.concatenate([block, jnp.zeros((128 - own, 128), jnp.float32)], axis=0)
        wt[pl.ds(at, 128), :] = block.T.astype(jnp.bfloat16)

    acc[...] = jnp.zeros_like(acc)
    pl.semaphore_wait(barrier, len(peers))

    for dz in ORDER:
        for dx in range(X):
            to_x = lax.rem(x + dx, X)
            to = p_of(to_x, zh + ZH - dz)
            slot = dz * X + x
            if dz or dx:
                send(con_ref.at[:, to], con_in.at[slot], sent_sem.at[0], con_sem.at[dz], to, me_j)
            else:
                pltpu.make_async_copy(con_ref.at[:, to], con_in.at[slot], con_sem.at[dz]).start()

    @pl.loop(0, NJ)
    def _(j):
        jz, jy, jc = j // (Y * CORES), lax.rem(j // CORES, Y), lax.rem(j, CORES)
        at = pl.multiple_of((jc * ZL + jz) * 128, 128)
        from_row = pl.multiple_of(j * own, 32)
        main = wt[pl.ds(from_row, own), :]
        for i in range(X - 1):
            spare = wt[pl.ds(pl.multiple_of(from_row + 32 * i, 32), 32), :]
            right[jy * (X - 1) + i, pl.ds(at, own), 0:128] = main
            right[jy * (X - 1) + i, pl.ds(at + own, 32), 0:128] = jnp.zeros_like(spare)
            right[jy * (X - 1) + i, pl.ds(at, own), 128:256] = jnp.zeros_like(main)
            right[jy * (X - 1) + i, pl.ds(at + own, 32), 128:256] = spare

    for q in range(NP):
        value = jnp.zeros((npc, nk * npv), jnp.int32)
        for k in range(nk):
            value = jnp.where(lane == k, table_ref[k, q], value)
        label[q] = value

    def onward(n, z, sy, up, down):
        slot = slot_of(sy, core, z, n)
        chunk = wide.at[slot]
        for go, d in ((up, 1), (down, Y - 1)):
            if go is not None:

                @pl.when(go)
                def _():
                    send(chunk, chunk, sent_sem.at[1], hop_sem.at[slot], me_p, j_of(zl, y + d, core))

        send(chunk, chunk, sent_sem.at[2], pair_sem.at[lax.rem(sy, Y)], me_p, j_of(zl, y, 1 - core))

    for n, dz in SEQUENCE:
        slot = slot_of(y, core, zl + dz, n)
        if dz == 0:
            wait(con_in.at[pl.ds(n * X, X)], con_sem.at[n])
            parts = [con_in[n * X + i].astype(jnp.float32).reshape(rows, own) for i in range(X)]
            for i in range(X - 1):
                packed = jnp.concatenate([parts[i], parts[X - 1][:, 32 * i : 32 * i + 32]], axis=1)
                wide[slot, i * rows : (i + 1) * rows, :] = packed.astype(jnp.bfloat16)
            for d in range(1, ZL):
                send(wide.at[slot], wide.at[slot], sent_sem.at[1], hop_sem.at[slot], me_p, j_of(zl + d, y, core))
        else:
            wait(wide.at[slot], hop_sem.at[slot])
        onward(n, zl + dz, y, True, True)

    for dz in ORDER:
        for dx in range(X):
            to = p_of(lax.rem(x + dx, X), zh + ZH - dz)
            slot = dz * X + x
            if dz or dx:
                send(val_ref.at[:, to], val_in.at[slot], sent_sem.at[3], val_sem, to, me_j)
            else:
                pltpu.make_async_copy(val_ref.at[:, to], val_in.at[slot], val_sem).start()

    def multiply(sy, i):
        left = [
            wide[pl.ds(slot_of(sy, c, z, 0), ZH), i * rows : (i + 1) * rows, :].reshape(ZH * rows, 128)
            for c in range(CORES)
            for z in range(ZL)
        ]
        acc[i] += jnp.dot(
            jnp.concatenate(left, axis=1), right[lax.rem(sy, Y) * (X - 1) + i], preferred_element_type=jnp.float32
        )

    def pair_ready(sy):
        wait(wide.at[pl.ds(slot_of(sy, 1 - core, 0, 0), ZL * ZH)], pair_sem.at[lax.rem(sy, Y)])

    @pl.loop(1, Y // 2 + 1)
    def _(t):
        below, above = y + Y - t, y + t
        for at, (n, dz) in enumerate(SEQUENCE):
            for sy, reach, up in ((below, REACH_UP[n], True), (above, REACH_DOWN[n], False)):

                @pl.when(t <= reach)
                def _():
                    slot = slot_of(sy, core, zl + dz, n)
                    wait(wide.at[slot], hop_sem.at[slot])
                    go = t < reach
                    onward(n, zl + dz, sy, go if up else None, None if up else go)

            if at % 2:
                i = at // 4
                if at % 4 == 1:
                    if i == 0:
                        pair_ready(below + 1)
                    multiply(below + 1, i)
                else:

                    @pl.when(t > 1)
                    def _():
                        if i == 0:
                            pair_ready(above + Y - 1)
                        multiply(above + Y - 1, i)

    pair_ready(y + Y // 2)
    for i in range(X - 1):
        multiply(y + Y // 2, i)

    wait(val_in, val_sem)
    for n in ORDER:
        for i in range(X):
            slot = n * X + i
            here = slice(n * rows, (n + 1) * rows)
            if i < X - 1:
                u = acc[i, here, 0:own]
            else:
                u = acc[0, here, 128 : 128 + own] + acc[1, here, 128 : 128 + own] + acc[2, here, 128 : 128 + own]
            high = u.astype(jnp.bfloat16)
            low = (u - high.astype(jnp.float32)).astype(jnp.bfloat16)
            both = lax.dot_general(
                jnp.concatenate([high, low], axis=0), val_in[slot].reshape(nk * npv, own),
                (((1,), (1,)), ((), ())), preferred_element_type=jnp.float32,
            )
            both = both[:rows] + both[rows:]
            tile = jnp.zeros((npc, nk * npv), jnp.float32)
            for k in range(nk):
                tile = jnp.where(lane == k, both[k * npc : (k + 1) * npc], tile)
            part[slot] = tile
            to_p = p_of(i, zh + n)
            to_j = j_of(1, to_p // CORES, lax.rem(to_p, CORES))

            @pl.when(to_j == me_j)
            def _():
                pltpu.make_async_copy(part.at[slot], tiles.at[me_j], tile_sem).start()

            @pl.when(to_j != me_j)
            def _():
                send(part.at[slot], tiles.at[me_j], sent_sem.at[4], tile_sem, me_p, to_j)

    @pl.when(zl == 1)
    def _():
        wait(tiles, tile_sem)
        sums = [tiles[j] for j in range(NJ)]
        while len(sums) > 1:
            sums = [a + b for a, b in zip(sums[::2], sums[1::2])] + sums[len(sums) // 2 * 2 :]
        total[...] = sums[0]
        to_p = y * CORES + core

        @pl.loop(0, NJ)
        def _(j):
            itself = (to_p == me_p) & (j == me_j)

            @pl.when(itself)
            def _():
                pltpu.make_async_copy(total, back.at[me_p], back_sem).start()

            @pl.when(jnp.logical_not(itself))
            def _():
                send(total, back.at[me_p], sent_sem.at[5], back_sem, to_p, j)

    wait(back, back_sem)
    for j in range(NP):
        chosen = jnp.zeros((npc, nk * npv), jnp.float32)
        for q in range(NP):
            chosen = jnp.where(label[q] == j, back[q], chosen)
        for k in range(nk):
            out_ref[k, j] = chosen[:, k * npv : (k + 1) * npv]

    hops = sum(REACH_UP + REACH_DOWN) * ZL + (ZL - 1) * ZH
    wait(con_in.at[pl.ds(0, NP - 1)], sent_sem.at[0])
    wait(wide.at[pl.ds(0, hops)], sent_sem.at[1])
    wait(wide.at[pl.ds(0, NJ // CORES * ZH)], sent_sem.at[2])
    wait(val_in.at[pl.ds(0, NP - 1)], sent_sem.at[3])
    adds_up = zl == 1

    @pl.when(adds_up)
    def _():
        wait(part.at[pl.ds(0, NP - 1)], sent_sem.at[4])

        @pl.when(y * CORES + core == me_p)
        def _():
            wait(tiles.at[pl.ds(0, NJ - 1)], sent_sem.at[5])

        @pl.when(y * CORES + core != me_p)
        def _():
            wait(tiles, sent_sem.at[5])

    @pl.when(jnp.logical_not(adds_up))
    def _():
        wait(part, sent_sem.at[4])


def per_device(valence, conduction, screened, kq_table):
    nk, nq, npv, own = valence.shape
    npc = conduction.shape[2]
    rows = nk * npc
    in_place = pl.BlockSpec(memory_space=pl.ANY)
    return pl.pallas_call(
        kernel,
        out_shape=jax.ShapeDtypeStruct((nk, nq, npc, npv), jnp.float32),
        in_specs=[
            in_place,
            in_place,
            pl.BlockSpec(memory_space=pltpu.VMEM),
            pl.BlockSpec(memory_space=pltpu.SMEM),
        ],
        out_specs=pl.BlockSpec(memory_space=pltpu.VMEM),
        scratch_shapes=[
            pltpu.VMEM((NP, nk, npc, own), jnp.bfloat16),
            pltpu.VMEM((NP, nk, npv, own), jnp.bfloat16),
            pltpu.VMEM((NJ * ZH, (X - 1) * rows, 128), jnp.bfloat16),
            pltpu.VMEM((Y * (X - 1), CORES * ZL * 128, 256), jnp.bfloat16),
            pltpu.VMEM((NJ * own, 128), jnp.bfloat16),
            pltpu.VMEM((X - 1, ZH * rows, 256), jnp.float32),
            pltpu.VMEM((NP, npc, nk * npv), jnp.float32),
            pltpu.VMEM((NJ, npc, nk * npv), jnp.float32),
            pltpu.VMEM((npc, nk * npv), jnp.float32),
            pltpu.VMEM((NP, npc, nk * npv), jnp.float32),
            pltpu.VMEM((NP, npc, nk * npv), jnp.int32),
            pltpu.SemaphoreType.DMA((ZH,)),
            pltpu.SemaphoreType.DMA,
            pltpu.SemaphoreType.DMA((NJ * ZH,)),
            pltpu.SemaphoreType.DMA((Y,)),
            pltpu.SemaphoreType.DMA,
            pltpu.SemaphoreType.DMA,
            pltpu.SemaphoreType.DMA((6,)),
        ],
        compiler_params=pltpu.CompilerParams(
            collective_id=0, has_side_effects=True, vmem_limit_bytes=48 * 1024 * 1024
        ),
    )(valence, conduction, screened, kq_table)


def solution(mesh):
    return jax.shard_map(
        per_device,
        mesh=mesh,
        in_specs=(
            P("pb", None, None, "ga"),
            P("pb", None, None, "ga"),
            P("pb", "ga", None),
            P("pb", None),
        ),
        out_specs=P("pb", None, None, None),
        check_vma=False,
    )
```

time: 555 us -> 89.1 us (0.16); the launches traced: 549 us -> 88.9 us
  blocking collectives: 286 us -> 0 us
  waiting for transfers between devices: 204 us -> 0 us
  Pallas kernels: 0 us -> 84.3 us
  local copies, waits for them, and re-layouts: 29.4 us -> 4.52 us
  between operations: 13.5 us -> 0.01 us
  matrix products: 9.47 us -> 0 us
    all_gather x1 -> x0, waiting for transfers between devices: 204 us -> none  [per_device(): lax.all_gather(valence_q, 'ga', axis=3, tiled=True)]
    psum x1 -> x0, blocking collectives: 180 us -> none  [per_device(): summed = lax.psum(partial_value, 'ga')]
    all_to_all x2 -> x0, blocking collectives: 106 us -> none  [the longest x1 74.1 us: per_device(): lax.all_to_all(summed, 'pb', split_axis=0, concat_axis=1, tiled=True)]
    pallas_call x0 -> x1, Pallas kernels: none -> 84.3 us  [per_device(): pl.pallas_call(kernel, out_shape=jax.ShapeDtypeStruct((nk, nq, npc, npv),...]
    all_gather x1 -> x0, local copies, waits for them, and re-layouts: 23.2 us -> none  [per_device(): lax.all_gather(valence_q, 'ga', axis=3, tiled=True)]
    dot_general x3 -> x0, matrix products: 9.47 us -> none  [the longest x1 8.33 us: per_device(): jnp.einsum('qgh,kqph->qgkp', screened, lax.all_gather(valence_q, 'ga', ax...]
  transfers between devices with their start and end apart: 2 -> 0, of which waited for: 1 -> 0; matrix products, arithmetic and copies ran while one was open for 6% -> 0% of each run, Pallas kernels for 0% -> 0%
where the time goes in v1:
time: 89.1 us; the launch traced here: 88.9 us
  Pallas kernels  84.3 us (95%)
  local copies, waits for them, and re-layouts  4.52 us (5%)
    pallas_call x1, Pallas kernels, per_device(): pl.pallas_call(kernel, out_shape=jax.ShapeDtypeStruct((nk, nq, npc, npv),...  84.3 us
    unnamed x9, local copies, waits for them, and re-layouts  4.52 us

profile of v1, /device:TPU:1, one launch (start us, length us, event | category | flops | bytes accessed | tf_op | source)
XLA Modules:
  0.0 88.9 jit_solution(9330867503756649307)
XLA Ops:
  0.0 0.0 copy-start
  0.0 1.2 %copy-done = bf16[1,96,4608]{2,1,0:T(8,128)(2,1)S(1)} copy-done((bf16[1,96,4608]{2,1,0:T(8,128)(2,1)S(1)}, bf16[1,96,4608]{2,1,0:T(8,128)(2,1)}, u32[]{:S(2)}) %copy-start) | copy-done | bytes 884760
  1.2 0.0 copy-start.1
  1.2 1.0 %copy-done.1 = bf16[6,16,16,96]{3,2,1,0:T(8,128)(2,1)S(1)} copy-done((bf16[6,16,16,96]{3,2,1,0:T(8,128)(2,1)S(1)}, bf16[6,16,16,96]{3,2,1,0:T(8,128)(2,1)}, u32[]{:S(2)}) %copy-start.1) | copy-done | bytes 294936
  2.2 0.0 copy-start.2
  2.2 0.9 %copy-done.2 = bf16[6,16,8,96]{3,2,1,0:T(8,128)(2,1)S(1)} copy-done((bf16[6,16,8,96]{3,2,1,0:T(8,128)(2,1)S(1)}, bf16[6,16,8,96]{3,2,1,0:T(8,128)(2,1)}, u32[]{:S(2)}) %copy-start.2) | copy-done | bytes 147480
  3.1 0.0 copy-start.3
  3.1 0.7 copy-done.3
  3.8 84.3 %shard_map.46 = f32[6,16,8,16]{3,2,1,0:T(8,128)S(1)} custom-call(bf16[6,16,16,96]{3,2,1,0:T(8,128)(2,1)S(1)} %copy-done.1, bf16[6,16,8,96]{3,2,1,0:T(8,128)(2,1)S(1)} %copy-done.2, bf16[1,96,4608]{2,1,0:T(8,128)(2,1)S(1)} %copy-done, s32[6,16]{1,0:T(8,128)S(1)} %copy-done.3), custom_call_target="tpu_custom_call" | custom-call | tf_op jit(solution)/shard_map/pallas_call | solution.py:271
  88.1 0.7 copy.6
Async XLA Ops:
  0.0 1.2 %copy-start = (bf16[1,96,4608]{2,1,0:T(8,128)(2,1)S(1)}, bf16[1,96,4608]{2,1,0:T(8,128)(2,1)}, u32[]{:S(2)}) copy-start(bf16[1,96,4608]{2,1,0:T(8,128)(2,1)} %w_ref.1) | copy-start | bytes 2654212
  1.2 1.0 %copy-start.1 = (bf16[6,16,16,96]{3,2,1,0:T(8,128)(2,1)S(1)}, bf16[6,16,16,96]{3,2,1,0:T(8,128)(2,1)}, u32[]{:S(2)}) copy-start(bf16[6,16,16,96]{3,2,1,0:T(8,128)(2,1)} %val_ref.1) | copy-start | bytes 884740
  2.2 0.9 %copy-start.2 = (bf16[6,16,8,96]{3,2,1,0:T(8,128)(2,1)S(1)}, bf16[6,16,8,96]{3,2,1,0:T(8,128)(2,1)}, u32[]{:S(2)}) copy-start(bf16[6,16,8,96]{3,2,1,0:T(8,128)(2,1)} %con_ref.1) | copy-start | bytes 442372
  3.1 0.7 copy-start.3

commit v2 on v0

v2 whole, which is shorter than its diff:
```python
import jax
import jax.numpy as jnp
from jax import lax
from jax.experimental import pallas as pl
from jax.experimental.pallas import tpu as pltpu
from jax.sharding import PartitionSpec as P

MESH = pl.DeviceIdType.MESH
X, ZH, ZL, Y, CORES = 4, 4, 3, 8, 2
NP, NJ = X * ZH, ZL * Y * CORES
NS = ZL * Y
REACH_UP = (4, 3, 3, 4)
REACH_DOWN = (3, 4, 4, 3)
PREPARE = 6


def kernel(
    val_ref, con_ref, w_hbm, table_hbm, out_ref,
    con_in, val_in, val_pair, wide, w_ref, table_ref, wt, wt_pair, acc, part, tiles, total, back, label,
    entered, con_sem, val_sem, val_pair_sem, wt_pair_sem, hop_sem, tile_sem, back_sem, sent_sem, load_sem,
):
    me_p, me_j = lax.axis_index("pb"), lax.axis_index("ga")
    x, zh = me_p // ZH, lax.rem(me_p, ZH)
    zl, y, core = me_j // (Y * CORES), lax.rem(me_j // CORES, Y), lax.rem(me_j, CORES)
    nk, _, npc, own = con_ref.shape
    npv = val_ref.shape[2]
    rows = nk * npc
    spare = 128 - own

    def p_of(px, pz):
        return px * ZH + lax.rem(pz, ZH)

    def j_of(jz, jy, jc):
        return (lax.rem(jz, ZL) * Y + lax.rem(jy, Y)) * CORES + jc

    def slot_of(sy, sz, n):
        return (lax.rem(sy, Y) * ZL + lax.rem(sz, ZL)) * ZH + n

    def send(src, dst, sent, arrived, p, j):
        pltpu.make_async_remote_copy(
            src_ref=src, dst_ref=dst, send_sem=sent, recv_sem=arrived, device_id=(p, j), device_id_type=MESH
        ).start()

    def wait(ref, sem):
        pltpu.make_async_copy(ref, ref, sem).wait()

    pair = j_of(zl, y, 1 - core)
    load_w = pltpu.make_async_copy(w_hbm.at[0], w_ref, load_sem.at[0])
    load_table = pltpu.make_async_copy(table_hbm, table_ref, load_sem.at[1])
    load_w.start()
    load_table.start()

    barrier = pltpu.get_barrier_semaphore()
    near = [(p_of(lax.rem(x + d, X), zh), me_j) for d in range(1, X)]
    near += [(me_p, j_of(zl + d, y, core)) for d in range(1, ZL)]
    near += [(me_p, j_of(zl, y + d, core)) for d in (1, Y - 1)] + [(me_p, pair)]
    for p, j in near:
        pl.semaphore_signal(barrier, inc=1, device_id=(p, j), device_id_type=MESH)
    for d in range(1, ZH):

        @pl.when(zh + d < ZH)
        def _():
            for to_x in range(X):
                pl.semaphore_signal(barrier, inc=1, device_id=(p_of(to_x, zh + d), me_j), device_id_type=MESH)

    acc[...] = jnp.zeros_like(acc)
    pl.semaphore_wait(barrier, len(near) + X * zh)

    def exchange(ref, into, sent, sem, d):
        slot = (ZH - d) % ZH * X + x
        for dx in range(X):
            to = p_of(lax.rem(x + dx, X), zh + d)
            if d or dx:
                send(ref.at[:, to], into.at[slot], sent_sem.at[sent], sem.at[(ZH - d) % ZH], to, me_j)
            else:
                pltpu.make_async_copy(ref.at[:, to], into.at[slot], sem.at[0]).start()

    exchange(con_ref, con_in, 0, con_sem, 0)
    for d in range(1, ZH):

        @pl.when(zh + d >= ZH)
        def _():
            for to_x in range(X):
                pl.semaphore_signal(
                    entered.at[ZH - d], inc=1, device_id=(p_of(to_x, zh + d), me_j), device_id_type=MESH
                )

    for d in (1, 3, 2):

        @pl.when(zh + d >= ZH)
        def _():
            exchange(con_ref, con_in, 0, con_sem, d)

    exchange(val_ref, val_in, 3, val_sem, 0)

    def upward():
        for d in range(1, ZH):

            @pl.when(zh + d < ZH)
            def _():
                pl.semaphore_wait(entered.at[d], X)
                exchange(con_ref, con_in, 0, con_sem, d)

    def valence_out():
        for d in (1, 3, 2):
            exchange(val_ref, val_in, 3, val_sem, d)

    def prepare(piece):
        if piece == 0:
            load_w.wait()
        tiles_each = w_ref.shape[1] // 128 // PREPARE

        @pl.loop(piece * tiles_each, (piece + 1) * tiles_each)
        def _(a):
            at = pl.multiple_of(a * 128, 128)
            block = w_ref[:, pl.ds(at, 128)].astype(jnp.float32)
            block = jnp.concatenate([block, jnp.zeros((spare, 128), jnp.float32)], axis=0).T.astype(jnp.bfloat16)
            for b in range(128 // 32):
                row = a * (128 // 32) + b
                wt[row // (own // 32), pl.ds(pl.multiple_of(lax.rem(row, own // 32) * 32, 32), 32), :] = block[32 * b : 32 * b + 32]

    def screened_out():
        by_core = wt.reshape(NS, CORES, own, 128)
        send(by_core.at[:, 1 - core], wt_pair, sent_sem.at[6], wt_pair_sem, me_p, pair)

    def labels():
        load_table.wait()
        lane = lax.broadcasted_iota(jnp.int32, (npc, nk * npv), 1) // npv
        for q in range(NP):
            value = jnp.zeros((npc, nk * npv), jnp.int32)
            for k in range(nk):
                value = jnp.where(lane == k, table_ref[k, q], value)
            label[q] = value

    def onward(slot, up, down):
        for go, d in ((up, 1), (down, Y - 1)):
            if go:
                send(wide.at[slot], wide.at[slot], sent_sem.at[1], hop_sem.at[slot], me_p, j_of(zl, y + d, core))

    def begin(n):
        slot = slot_of(y, zl, n)
        wait(con_in.at[pl.ds(n * X, X)], con_sem.at[n])
        parts = [con_in[n * X + i].astype(jnp.float32).reshape(rows, own) for i in range(X)]
        for i in range(X - 1):
            packed = jnp.concatenate([parts[i], parts[X - 1][:, spare * i : spare * (i + 1)]], axis=1)
            wide[slot, i * rows : (i + 1) * rows, :] = packed.astype(jnp.bfloat16)
        for d in range(1, ZL):
            send(wide.at[slot], wide.at[slot], sent_sem.at[1], hop_sem.at[slot], me_p, j_of(zl + d, y, core))
        onward(slot, True, True)

    def hop(n, t):
        for dz in range(ZL):
            if t == 0 and dz:
                slot = slot_of(y, zl + dz, n)
                wait(wide.at[slot], hop_sem.at[slot])
                onward(slot, True, True)
            if t:
                for sy, reach, up in ((y + Y - t, REACH_UP[n], True), (y + t, REACH_DOWN[n], False)):
                    if t <= reach:
                        slot = slot_of(sy, zl + dz, n)
                        wait(wide.at[slot], hop_sem.at[slot])
                        onward(slot, up and t < reach, not up and t < reach)

    def multiply(n, t):
        for sy in [y + t] if t in (0, Y // 2) else [y + Y - t, y + t]:
            left, right = [], []
            for z in range(ZL):
                chunk = wide[slot_of(sy, z, n)]
                thirds = [chunk[i * rows : (i + 1) * rows].astype(jnp.float32) for i in range(X - 1)]
                fourth = jnp.concatenate([third[:, own:] for third in thirds] + [thirds[0][:, own:]], axis=1)
                left.append(jnp.concatenate([chunk, fourth.astype(jnp.bfloat16)], axis=0))
                source = z * Y + lax.rem(sy, Y)
                both = jnp.concatenate([wt[source * CORES + core], wt_pair[source]], axis=1)
                right += [both, jnp.zeros((spare, 256), jnp.bfloat16)]
            product = jnp.dot(
                jnp.concatenate(left, axis=1), jnp.concatenate(right, axis=0), preferred_element_type=jnp.float32
            )
            acc[...] = product if t == 0 else acc[...] + product

    def valence_pair(n):
        here = pl.ds(n * X, X)
        wait(val_in.at[here], val_sem.at[n])
        send(val_in.at[here], val_pair.at[here], sent_sem.at[2], val_pair_sem.at[n], me_p, pair)

    def second(n):
        wait(val_pair.at[pl.ds(n * X, X)], val_pair_sem.at[n])
        lane = lax.broadcasted_iota(jnp.int32, (npc, nk * npv), 1) // npv
        for i in range(X):
            u = acc[i * rows : (i + 1) * rows, :]
            high = u.astype(jnp.bfloat16)
            low = (u - high.astype(jnp.float32)).astype(jnp.bfloat16)
            stacked = jnp.concatenate([high, low], axis=0)
            both = sum(
                lax.dot_general(
                    stacked[:, at : at + own], from_[n * X + i].reshape(nk * npv, own),
                    (((1,), (1,)), ((), ())), preferred_element_type=jnp.float32,
                )
                for at, from_ in ((0, val_in), (128, val_pair))
            )
            both = both[:rows] + both[rows:]
            tile = jnp.zeros((npc, nk * npv), jnp.float32)
            for k in range(nk):
                tile = jnp.where(lane == k, both[k * npc : (k + 1) * npc], tile)
            part[n * X + i] = tile
        for i in range(X):
            to_p = p_of(i, zh + n)
            to_j = j_of(1, to_p // CORES, lax.rem(to_p, CORES))

            @pl.when(to_j == me_j)
            def _():
                pltpu.make_async_copy(part.at[n * X + i], tiles.at[me_j], tile_sem).start()

            @pl.when(to_j != me_j)
            def _():
                send(part.at[n * X + i], tiles.at[me_j], sent_sem.at[4], tile_sem, me_p, to_j)

    adds_for = y * CORES + core

    def add_up(n):
        @pl.when((zl == 1) & (lax.rem(adds_for + ZH - zh, ZH) == n))
        def _():
            wait(tiles, tile_sem)
            sums = [tiles[j] for j in range(NJ)]
            while len(sums) > 1:
                sums = [a + b for a, b in zip(sums[::2], sums[1::2])] + sums[len(sums) // 2 * 2 :]
            total[...] = sums[0]

            @pl.loop(0, NJ)
            def _(j):
                itself = (adds_for == me_p) & (j == me_j)

                @pl.when(itself)
                def _():
                    pltpu.make_async_copy(total, back.at[me_p], back_sem).start()

                @pl.when(jnp.logical_not(itself))
                def _():
                    send(total, back.at[me_p], sent_sem.at[5], back_sem, adds_for, j)

    def screened_ready():
        wait(wt_pair, wt_pair_sem)

    for step in (
        (begin, 0), (prepare, 0), (prepare, 1), (hop, 0, 0), (upward,), (prepare, 2), (prepare, 3), (hop, 0, 1),
        (prepare, 4), (prepare, 5), (screened_out,), (valence_out,), (begin, 1), (hop, 0, 2), (labels,), (hop, 1, 0),
        (hop, 0, 3), (valence_pair, 0), (screened_ready,), (multiply, 0, 0), (hop, 1, 1), (multiply, 0, 1), (hop, 0, 4),
        (multiply, 0, 2), (hop, 1, 2), (multiply, 0, 3), (multiply, 0, 4), (begin, 3), (second, 0), (hop, 3, 0),
        (multiply, 1, 0), (hop, 1, 3), (multiply, 1, 1), (valence_pair, 1), (hop, 3, 1), (multiply, 1, 2), (hop, 1, 4),
        (multiply, 1, 3), (hop, 3, 2), (multiply, 1, 4), (begin, 2), (second, 1), (add_up, 0), (hop, 2, 0),
        (multiply, 3, 0), (hop, 3, 3), (multiply, 3, 1), (valence_pair, 3), (hop, 2, 1), (multiply, 3, 2), (hop, 3, 4),
        (multiply, 3, 3), (multiply, 3, 4), (hop, 2, 2), (second, 3), (multiply, 2, 0), (add_up, 1), (hop, 2, 3),
        (multiply, 2, 1), (multiply, 2, 2), (valence_pair, 2), (add_up, 3), (hop, 2, 4), (multiply, 2, 3),
        (multiply, 2, 4), (second, 2), (add_up, 2),
    ):
        step[0](*step[1:])

    wait(back, back_sem)
    for j in range(NP):
        chosen = jnp.zeros((npc, nk * npv), jnp.float32)
        for q in range(NP):
            chosen = jnp.where(label[q] == j, back[q], chosen)
        for k in range(nk):
            out_ref[k, j] = chosen[:, k * npv : (k + 1) * npv]

    hops = sum(REACH_UP + REACH_DOWN) * ZL + (ZL - 1) * ZH
    wait(con_in.at[pl.ds(0, NP - 1)], sent_sem.at[0])
    wait(wide.at[pl.ds(0, hops)], sent_sem.at[1])
    wait(val_in, sent_sem.at[2])
    wait(val_in.at[pl.ds(0, NP - 1)], sent_sem.at[3])
    wait(wt_pair, sent_sem.at[6])

    @pl.when(zl == 1)
    def _():
        wait(part.at[pl.ds(0, NP - 1)], sent_sem.at[4])

        @pl.when(adds_for == me_p)
        def _():
            wait(tiles.at[pl.ds(0, NJ - 1)], sent_sem.at[5])

        @pl.when(adds_for != me_p)
        def _():
            wait(tiles, sent_sem.at[5])

    @pl.when(zl != 1)
    def _():
        wait(part, sent_sem.at[4])


def per_device(valence, conduction, screened, kq_table):
    nk, nq, npv, own = valence.shape
    npc = conduction.shape[2]
    rows = nk * npc
    return pl.pallas_call(
        kernel,
        out_shape=jax.ShapeDtypeStruct((nk, nq, npc, npv), jnp.float32),
        in_specs=[pl.BlockSpec(memory_space=pltpu.HBM)] * 4,
        out_specs=pl.BlockSpec(memory_space=pltpu.VMEM),
        scratch_shapes=[
            pltpu.VMEM((NP, nk, npc, own), jnp.bfloat16),
            pltpu.VMEM((NP, nk, npv, own), jnp.bfloat16),
            pltpu.VMEM((NP, nk, npv, own), jnp.bfloat16),
            pltpu.VMEM((NS * ZH, (X - 1) * rows, 128), jnp.bfloat16),
            pltpu.VMEM((own, NJ * own), jnp.bfloat16),
            pltpu.SMEM((nk, nq), jnp.int32),
            pltpu.VMEM((NJ, own, 128), jnp.bfloat16),
            pltpu.VMEM((NS, own, 128), jnp.bfloat16),
            pltpu.VMEM((X * rows, 256), jnp.float32),
            pltpu.VMEM((NP, npc, nk * npv), jnp.float32),
            pltpu.VMEM((NJ, npc, nk * npv), jnp.float32),
            pltpu.VMEM((npc, nk * npv), jnp.float32),
            pltpu.VMEM((NP, npc, nk * npv), jnp.float32),
            pltpu.VMEM((NP, npc, nk * npv), jnp.int32),
            pltpu.SemaphoreType.REGULAR((ZH,)),
            pltpu.SemaphoreType.DMA((ZH,)),
            pltpu.SemaphoreType.DMA((ZH,)),
            pltpu.SemaphoreType.DMA((ZH,)),
            pltpu.SemaphoreType.DMA,
            pltpu.SemaphoreType.DMA((NS * ZH,)),
            pltpu.SemaphoreType.DMA,
            pltpu.SemaphoreType.DMA,
            pltpu.SemaphoreType.DMA((7,)),
            pltpu.SemaphoreType.DMA((2,)),
        ],
        compiler_params=pltpu.CompilerParams(collective_id=0, has_side_effects=True, vmem_limit_bytes=67043328),
    )(valence, conduction, screened, kq_table)


def solution(mesh):
    return jax.shard_map(
        per_device,
        mesh=mesh,
        in_specs=(
            P("pb", None, None, "ga"),
            P("pb", None, None, "ga"),
            P("pb", "ga", None),
            P("pb", None),
        ),
        out_specs=P("pb", None, None, None),
        check_vma=False,
    )
```

time: 555 us -> 104 us (0.19)
  blocking collectives: 286 us -> 0 us
  waiting for transfers between devices: 204 us -> 0 us
  Pallas kernels: 0 us -> 101 us
  local copies, waits for them, and re-layouts: 29.4 us -> 1.77 us
  between operations: 13.5 us -> 0.01 us
  matrix products: 9.47 us -> 0 us
    all_gather x1 -> x0, waiting for transfers between devices: 204 us -> none  [per_device(): lax.all_gather(valence_q, 'ga', axis=3, tiled=True)]
    psum x1 -> x0, blocking collectives: 180 us -> none  [per_device(): summed = lax.psum(partial_value, 'ga')]
    all_to_all x2 -> x0, blocking collectives: 106 us -> none  [the longest x1 74.1 us: per_device(): lax.all_to_all(summed, 'pb', split_axis=0, concat_axis=1, tiled=True)]
    pallas_call x0 -> x1, Pallas kernels: none -> 101 us  [per_device(): pl.pallas_call(kernel, out_shape=jax.ShapeDtypeStruct((nk, nq, npc, npv),...]
    all_gather x1 -> x0, local copies, waits for them, and re-layouts: 23.2 us -> none  [per_device(): lax.all_gather(valence_q, 'ga', axis=3, tiled=True)]
    dot_general x3 -> x0, matrix products: 9.47 us -> none  [the longest x1 8.33 us: per_device(): jnp.einsum('qgh,kqph->qgkp', screened, lax.all_gather(valence_q, 'ga', ax...]
  transfers between devices with their start and end apart: 2 -> 0, of which waited for: 1 -> 0; matrix products, arithmetic and copies ran while one was open for 6% -> 0% of each run, Pallas kernels for 0% -> 0%
where the time goes in v2:
time: 104 us; the launch traced here: 103 us
  Pallas kernels  101 us (97%)
  local copies, waits for them, and re-layouts  1.77 us (2%)
    pallas_call x1, Pallas kernels, per_device(): pl.pallas_call(kernel, out_shape=jax.ShapeDtypeStruct((nk, nq, npc, npv),...  101 us

profile of v2, /device:TPU:1, one launch (start us, length us, event | category | flops | bytes accessed | tf_op | source)
XLA Modules:
  0.0 102.7 jit_solution(6631425402722259702)
XLA Ops:
  0.0 100.9 %shard_map.46 = f32[6,16,8,16]{3,2,1,0:T(8,128)} custom-call(bf16[6,16,16,96]{3,2,1,0:T(8,128)(2,1)} %val_ref.1, bf16[6,16,8,96]{3,2,1,0:T(8,128)(2,1)} %con_ref.1, bf16[1,96,4608]{2,1,0:T(8,128)(2,1)} %w_hbm.1, s32[6,16]{1,0:T(8,128)} %table_hbm.1), custom_call_target="tpu_custom_call" | custom-call | tf_op jit(solution)/shard_map/pallas_call | solution.py:293
  100.9 1.8 %copy.6 = f32[6,16,8,16]{3,2,1,0:T(8,128)} copy(f32[6,16,8,16]{3,2,1,0:T(8,128)} %shard_map.46) | data formatting | bytes 98304

commit v3 on v2

--- a/solution.py
+++ b/solution.py
@@ -17,7 +17,7 @@
 def kernel(
     val_ref, con_ref, w_hbm, table_hbm, out_ref,
     con_in, val_in, val_pair, wide, w_ref, table_ref, wt, wt_pair, acc, part, tiles, total, back, label,
-    entered, con_sem, val_sem, val_pair_sem, wt_pair_sem, hop_sem, tile_sem, back_sem, sent_sem, load_sem,
+    con_sem, val_sem, val_pair_sem, wt_pair_sem, hop_sem, tile_sem, back_sem, sent_sem, load_sem,
 ):
     me_p, me_j = lax.axis_index("pb"), lax.axis_index("ga")
     x, zh = me_p // ZH, lax.rem(me_p, ZH)
@@ -51,20 +51,12 @@
     load_table.start()
 
     barrier = pltpu.get_barrier_semaphore()
-    near = [(p_of(lax.rem(x + d, X), zh), me_j) for d in range(1, X)]
+    near = [(p_of(lax.rem(x + dx, X), zh + d), me_j) for d in range(ZH) for dx in range(X) if d or dx]
     near += [(me_p, j_of(zl + d, y, core)) for d in range(1, ZL)]
     near += [(me_p, j_of(zl, y + d, core)) for d in (1, Y - 1)] + [(me_p, pair)]
     for p, j in near:
         pl.semaphore_signal(barrier, inc=1, device_id=(p, j), device_id_type=MESH)
-    for d in range(1, ZH):
-
-        @pl.when(zh + d < ZH)
-        def _():
-            for to_x in range(X):
-                pl.semaphore_signal(barrier, inc=1, device_id=(p_of(to_x, zh + d), me_j), device_id_type=MESH)
-
-    acc[...] = jnp.zeros_like(acc)
-    pl.semaphore_wait(barrier, len(near) + X * zh)
+    pl.semaphore_wait(barrier, len(near))
 
     def exchange(ref, into, sent, sem, d):
         slot = (ZH - d) % ZH * X + x
@@ -75,34 +67,11 @@
             else:
                 pltpu.make_async_copy(ref.at[:, to], into.at[slot], sem.at[0]).start()
 
-    exchange(con_ref, con_in, 0, con_sem, 0)
-    for d in range(1, ZH):
-
-        @pl.when(zh + d >= ZH)
-        def _():
-            for to_x in range(X):
-                pl.semaphore_signal(
-                    entered.at[ZH - d], inc=1, device_id=(p_of(to_x, zh + d), me_j), device_id_type=MESH
-                )
-
-    for d in (1, 3, 2):
-
-        @pl.when(zh + d >= ZH)
-        def _():
-            exchange(con_ref, con_in, 0, con_sem, d)
-
-    exchange(val_ref, val_in, 3, val_sem, 0)
-
-    def upward():
-        for d in range(1, ZH):
-
-            @pl.when(zh + d < ZH)
-            def _():
-                pl.semaphore_wait(entered.at[d], X)
-                exchange(con_ref, con_in, 0, con_sem, d)
+    for d in (0, 1, 3, 2):
+        exchange(con_ref, con_in, 0, con_sem, d)
 
     def valence_out():
-        for d in (1, 3, 2):
+        for d in (0, 1, 3, 2):
             exchange(val_ref, val_in, 3, val_sem, d)
 
     def prepare(piece):
@@ -175,7 +144,7 @@
             product = jnp.dot(
                 jnp.concatenate(left, axis=1), jnp.concatenate(right, axis=0), preferred_element_type=jnp.float32
             )
-            acc[...] = product if t == 0 else acc[...] + product
+            acc[n] = product if t == 0 else acc[n] + product
 
     def valence_pair(n):
         here = pl.ds(n * X, X)
@@ -186,7 +155,7 @@
         wait(val_pair.at[pl.ds(n * X, X)], val_pair_sem.at[n])
         lane = lax.broadcasted_iota(jnp.int32, (npc, nk * npv), 1) // npv
         for i in range(X):
-            u = acc[i * rows : (i + 1) * rows, :]
+            u = acc[n, i * rows : (i + 1) * rows, :]
             high = u.astype(jnp.bfloat16)
             low = (u - high.astype(jnp.float32)).astype(jnp.bfloat16)
             stacked = jnp.concatenate([high, low], axis=0)
@@ -241,16 +210,16 @@
         wait(wt_pair, wt_pair_sem)
 
     for step in (
-        (begin, 0), (prepare, 0), (prepare, 1), (hop, 0, 0), (upward,), (prepare, 2), (prepare, 3), (hop, 0, 1),
-        (prepare, 4), (prepare, 5), (screened_out,), (valence_out,), (begin, 1), (hop, 0, 2), (labels,), (hop, 1, 0),
-        (hop, 0, 3), (valence_pair, 0), (screened_ready,), (multiply, 0, 0), (hop, 1, 1), (multiply, 0, 1), (hop, 0, 4),
-        (multiply, 0, 2), (hop, 1, 2), (multiply, 0, 3), (multiply, 0, 4), (begin, 3), (second, 0), (hop, 3, 0),
-        (multiply, 1, 0), (hop, 1, 3), (multiply, 1, 1), (valence_pair, 1), (hop, 3, 1), (multiply, 1, 2), (hop, 1, 4),
-        (multiply, 1, 3), (hop, 3, 2), (multiply, 1, 4), (begin, 2), (second, 1), (add_up, 0), (hop, 2, 0),
-        (multiply, 3, 0), (hop, 3, 3), (multiply, 3, 1), (valence_pair, 3), (hop, 2, 1), (multiply, 3, 2), (hop, 3, 4),
-        (multiply, 3, 3), (multiply, 3, 4), (hop, 2, 2), (second, 3), (multiply, 2, 0), (add_up, 1), (hop, 2, 3),
-        (multiply, 2, 1), (multiply, 2, 2), (valence_pair, 2), (add_up, 3), (hop, 2, 4), (multiply, 2, 3),
-        (multiply, 2, 4), (second, 2), (add_up, 2),
+        (begin, 0), (prepare, 0), (begin, 1), (prepare, 1), (hop, 0, 0), (begin, 3), (prepare, 2), (hop, 1, 0), (begin, 2),
+        (prepare, 3), (hop, 3, 0), (prepare, 4), (hop, 2, 0), (valence_out,), (prepare, 5), (screened_out,), (labels,),
+        (hop, 0, 1), (hop, 1, 1), (hop, 3, 1), (hop, 2, 1), (screened_ready,),
+        (hop, 0, 2), (multiply, 0, 0), (multiply, 1, 0), (hop, 1, 2), (multiply, 3, 0), (multiply, 2, 0), (hop, 3, 2),
+        (multiply, 0, 1), (hop, 2, 2), (multiply, 1, 1), (hop, 0, 3), (multiply, 3, 1), (multiply, 2, 1), (hop, 1, 3),
+        (multiply, 0, 2), (multiply, 1, 2), (hop, 3, 3), (multiply, 3, 2), (hop, 2, 3), (multiply, 2, 2), (valence_pair, 0),
+        (valence_pair, 1), (valence_pair, 3), (valence_pair, 2), (hop, 0, 4),
+        (multiply, 0, 3), (multiply, 0, 4), (hop, 1, 4), (multiply, 1, 3), (multiply, 1, 4), (second, 0),
+        (hop, 3, 4), (multiply, 3, 3), (multiply, 3, 4), (second, 1), (hop, 2, 4), (multiply, 2, 3), (multiply, 2, 4),
+        (second, 3), (second, 2), (add_up, 0), (add_up, 1), (add_up, 3), (add_up, 2),
     ):
         step[0](*step[1:])
 
@@ -304,13 +273,12 @@
             pltpu.SMEM((nk, nq), jnp.int32),
             pltpu.VMEM((NJ, own, 128), jnp.bfloat16),
             pltpu.VMEM((NS, own, 128), jnp.bfloat16),
-            pltpu.VMEM((X * rows, 256), jnp.float32),
+            pltpu.VMEM((ZH, X * rows, 256), jnp.float32),
             pltpu.VMEM((NP, npc, nk * npv), jnp.float32),
             pltpu.VMEM((NJ, npc, nk * npv), jnp.float32),
             pltpu.VMEM((npc, nk * npv), jnp.float32),
             pltpu.VMEM((NP, npc, nk * npv), jnp.float32),
             pltpu.VMEM((NP, npc, nk * npv), jnp.int32),
-            pltpu.SemaphoreType.REGULAR((ZH,)),
             pltpu.SemaphoreType.DMA((ZH,)),
             pltpu.SemaphoreType.DMA((ZH,)),
             pltpu.SemaphoreType.DMA((ZH,)),

time: 104 us -> 82.3 us (0.79)
  Pallas kernels: 101 us -> 80.1 us
    pallas_call x1, Pallas kernels: 101 us -> 80.1 us  [per_device(): pl.pallas_call(kernel, out_shape=jax.ShapeDtypeStruct((nk, nq, npc, npv),...]
where the time goes in v3:
time: 82.3 us; the launch traced here: 81.9 us
  Pallas kernels  80.1 us (97%)
  local copies, waits for them, and re-layouts  1.77 us (2%)
    pallas_call x1, Pallas kernels, per_device(): pl.pallas_call(kernel, out_shape=jax.ShapeDtypeStruct((nk, nq, npc, npv),...  80.1 us
    unnamed x1, local copies, waits for them, and re-layouts  1.77 us

profile of v3, /device:TPU:1, one launch (start us, length us, event | category | flops | bytes accessed | tf_op | source)
XLA Modules:
  0.0 81.9 jit_solution(14156335992686415816)
XLA Ops:
  0.0 80.1 %shard_map.46 = f32[6,16,8,16]{3,2,1,0:T(8,128)} custom-call(bf16[6,16,16,96]{3,2,1,0:T(8,128)(2,1)} %val_ref.1, bf16[6,16,8,96]{3,2,1,0:T(8,128)(2,1)} %con_ref.1, bf16[1,96,4608]{2,1,0:T(8,128)(2,1)} %w_hbm.1, s32[6,16]{1,0:T(8,128)} %table_hbm.1), custom_call_target="tpu_custom_call" | custom-call | tf_op jit(solution)/shard_map/pallas_call | solution.py:262
  80.1 1.8 %copy.6 = f32[6,16,8,16]{3,2,1,0:T(8,128)} copy(f32[6,16,8,16]{3,2,1,0:T(8,128)} %shard_map.46) | data formatting | bytes 98304

commit v4 on v3

--- a/solution.py
+++ b/solution.py
@@ -117,20 +117,25 @@
             send(wide.at[slot], wide.at[slot], sent_sem.at[1], hop_sem.at[slot], me_p, j_of(zl + d, y, core))
         onward(slot, True, True)
 
-    def hop(n, t):
+    def enter(n):
+        for dz in range(1, ZL):
+            slot = slot_of(y, zl + dz, n)
+            wait(wide.at[slot], hop_sem.at[slot])
+            onward(slot, True, True)
+
+    def offset(row):
+        return lax.rem(row + ZH - zh, ZH)
+
+    def hop(row, t):
         for dz in range(ZL):
-            if t == 0 and dz:
-                slot = slot_of(y, zl + dz, n)
-                wait(wide.at[slot], hop_sem.at[slot])
-                onward(slot, True, True)
-            if t:
-                for sy, reach, up in ((y + Y - t, REACH_UP[n], True), (y + t, REACH_DOWN[n], False)):
-                    if t <= reach:
-                        slot = slot_of(sy, zl + dz, n)
-                        wait(wide.at[slot], hop_sem.at[slot])
-                        onward(slot, up and t < reach, not up and t < reach)
-
-    def multiply(n, t):
+            for sy, reach, up in ((y + Y - t, REACH_UP[row], True), (y + t, REACH_DOWN[row], False)):
+                if t <= reach:
+                    slot = slot_of(sy, zl + dz, offset(row))
+                    wait(wide.at[slot], hop_sem.at[slot])
+                    onward(slot, up and t < reach, not up and t < reach)
+
+    def multiply(row, t):
+        n = offset(row)
         for sy in [y + t] if t in (0, Y // 2) else [y + Y - t, y + t]:
             left, right = [], []
             for z in range(ZL):
@@ -146,12 +151,14 @@
             )
             acc[n] = product if t == 0 else acc[n] + product
 
-    def valence_pair(n):
+    def valence_pair(row):
+        n = offset(row)
         here = pl.ds(n * X, X)
         wait(val_in.at[here], val_sem.at[n])
         send(val_in.at[here], val_pair.at[here], sent_sem.at[2], val_pair_sem.at[n], me_p, pair)
 
-    def second(n):
+    def second(row):
+        n = offset(row)
         wait(val_pair.at[pl.ds(n * X, X)], val_pair_sem.at[n])
         lane = lax.broadcasted_iota(jnp.int32, (npc, nk * npv), 1) // npv
         for i in range(X):
@@ -172,7 +179,7 @@
                 tile = jnp.where(lane == k, both[k * npc : (k + 1) * npc], tile)
             part[n * X + i] = tile
         for i in range(X):
-            to_p = p_of(i, zh + n)
+            to_p = p_of(i, row)
             to_j = j_of(1, to_p // CORES, lax.rem(to_p, CORES))
 
             @pl.when(to_j == me_j)
@@ -185,8 +192,8 @@
 
     adds_for = y * CORES + core
 
-    def add_up(n):
-        @pl.when((zl == 1) & (lax.rem(adds_for + ZH - zh, ZH) == n))
+    def add_up(row):
+        @pl.when((zl == 1) & (lax.rem(adds_for, ZH) == row))
         def _():
             wait(tiles, tile_sem)
             sums = [tiles[j] for j in range(NJ)]
@@ -210,16 +217,16 @@
         wait(wt_pair, wt_pair_sem)
 
     for step in (
-        (begin, 0), (prepare, 0), (begin, 1), (prepare, 1), (hop, 0, 0), (begin, 3), (prepare, 2), (hop, 1, 0), (begin, 2),
-        (prepare, 3), (hop, 3, 0), (prepare, 4), (hop, 2, 0), (valence_out,), (prepare, 5), (screened_out,), (labels,),
-        (hop, 0, 1), (hop, 1, 1), (hop, 3, 1), (hop, 2, 1), (screened_ready,),
-        (hop, 0, 2), (multiply, 0, 0), (multiply, 1, 0), (hop, 1, 2), (multiply, 3, 0), (multiply, 2, 0), (hop, 3, 2),
-        (multiply, 0, 1), (hop, 2, 2), (multiply, 1, 1), (hop, 0, 3), (multiply, 3, 1), (multiply, 2, 1), (hop, 1, 3),
-        (multiply, 0, 2), (multiply, 1, 2), (hop, 3, 3), (multiply, 3, 2), (hop, 2, 3), (multiply, 2, 2), (valence_pair, 0),
-        (valence_pair, 1), (valence_pair, 3), (valence_pair, 2), (hop, 0, 4),
-        (multiply, 0, 3), (multiply, 0, 4), (hop, 1, 4), (multiply, 1, 3), (multiply, 1, 4), (second, 0),
-        (hop, 3, 4), (multiply, 3, 3), (multiply, 3, 4), (second, 1), (hop, 2, 4), (multiply, 2, 3), (multiply, 2, 4),
-        (second, 3), (second, 2), (add_up, 0), (add_up, 1), (add_up, 3), (add_up, 2),
+        (begin, 0), (prepare, 0), (begin, 1), (prepare, 1), (enter, 0), (begin, 3), (prepare, 2), (enter, 1), (begin, 2),
+        (prepare, 3), (enter, 3), (prepare, 4), (enter, 2), (valence_out,), (prepare, 5), (screened_out,), (labels,),
+        (hop, 0, 1), (hop, 1, 1), (hop, 2, 1), (hop, 3, 1), (screened_ready,),
+        (hop, 0, 2), (multiply, 0, 0), (multiply, 1, 0), (hop, 1, 2), (multiply, 2, 0), (multiply, 3, 0), (hop, 2, 2),
+        (multiply, 0, 1), (hop, 3, 2), (multiply, 1, 1), (hop, 0, 3), (multiply, 2, 1), (multiply, 3, 1), (hop, 1, 3),
+        (multiply, 0, 2), (multiply, 1, 2), (hop, 2, 3), (multiply, 2, 2), (hop, 3, 3), (multiply, 3, 2), (valence_pair, 0),
+        (valence_pair, 1), (valence_pair, 2), (valence_pair, 3), (hop, 0, 4),
+        (multiply, 0, 3), (multiply, 0, 4), (second, 0), (hop, 1, 4), (multiply, 1, 3), (multiply, 1, 4), (second, 1),
+        (hop, 2, 4), (multiply, 2, 3), (multiply, 2, 4), (second, 2), (hop, 3, 4), (multiply, 3, 3), (multiply, 3, 4),
+        (second, 3), (add_up, 0), (add_up, 1), (add_up, 2), (add_up, 3),
     ):
         step[0](*step[1:])
 

time: 82.3 us -> 81.7 us (level)
  no operation moved by 1% of the time
where the time goes in v4:
time: 81.7 us; the launch traced here: 81.6 us
  Pallas kernels  79.8 us (98%)
  local copies, waits for them, and re-layouts  1.77 us (2%)
    pallas_call x1, Pallas kernels, per_device(): pl.pallas_call(kernel, out_shape=jax.ShapeDtypeStruct((nk, nq, npc, npv),...  79.8 us
    unnamed x1, local copies, waits for them, and re-layouts  1.77 us

profile of v4, /device:TPU:1, one launch (start us, length us, event | category | flops | bytes accessed | tf_op | source)
XLA Modules:
  0.0 81.6 jit_solution(13757242149461770257)
XLA Ops:
  0.0 79.8 %shard_map.46 = f32[6,16,8,16]{3,2,1,0:T(8,128)} custom-call(bf16[6,16,16,96]{3,2,1,0:T(8,128)(2,1)} %val_ref.1, bf16[6,16,8,96]{3,2,1,0:T(8,128)(2,1)} %con_ref.1, bf16[1,96,4608]{2,1,0:T(8,128)(2,1)} %w_hbm.1, s32[6,16]{1,0:T(8,128)} %table_hbm.1), custom_call_target="tpu_custom_call" | custom-call | tf_op jit(solution)/shard_map/pallas_call | solution.py:269
  79.8 1.8 %copy.6 = f32[6,16,8,16]{3,2,1,0:T(8,128)} copy(f32[6,16,8,16]{3,2,1,0:T(8,128)} %shard_map.46) | data formatting | bytes 98304

commit v5 on v4

--- a/solution.py
+++ b/solution.py
@@ -217,9 +217,9 @@
         wait(wt_pair, wt_pair_sem)
 
     for step in (
-        (begin, 0), (prepare, 0), (begin, 1), (prepare, 1), (enter, 0), (begin, 3), (prepare, 2), (enter, 1), (begin, 2),
-        (prepare, 3), (enter, 3), (prepare, 4), (enter, 2), (valence_out,), (prepare, 5), (screened_out,), (labels,),
-        (hop, 0, 1), (hop, 1, 1), (hop, 2, 1), (hop, 3, 1), (screened_ready,),
+        (begin, 0), (begin, 1), (enter, 0), (begin, 3), (enter, 1), (begin, 2), (prepare, 0),
+        (enter, 3), (prepare, 1), (enter, 2), (prepare, 2), (prepare, 3), (prepare, 4), (prepare, 5), (screened_out,), (labels,),
+        (hop, 0, 1), (hop, 1, 1), (hop, 2, 1), (hop, 3, 1), (valence_out,), (screened_ready,),
         (hop, 0, 2), (multiply, 0, 0), (multiply, 1, 0), (hop, 1, 2), (multiply, 2, 0), (multiply, 3, 0), (hop, 2, 2),
         (multiply, 0, 1), (hop, 3, 2), (multiply, 1, 1), (hop, 0, 3), (multiply, 2, 1), (multiply, 3, 1), (hop, 1, 3),
         (multiply, 0, 2), (multiply, 1, 2), (hop, 2, 3), (multiply, 2, 2), (hop, 3, 3), (multiply, 3, 2), (valence_pair, 0),

time: 81.7 us -> 81.7 us (level)
  no operation moved by 1% of the time
where the time goes in v5:
time: 81.7 us; the launch traced here: 81.1 us
  Pallas kernels  79.3 us (97%)
  local copies, waits for them, and re-layouts  1.77 us (2%)
    pallas_call x1, Pallas kernels, per_device(): pl.pallas_call(kernel, out_shape=jax.ShapeDtypeStruct((nk, nq, npc, npv),...  79.3 us
    unnamed x1, local copies, waits for them, and re-layouts  1.77 us

profile of v5, /device:TPU:1, one launch (start us, length us, event | category | flops | bytes accessed | tf_op | source)
XLA Modules:
  0.0 81.1 jit_solution(17716470496954813660)
XLA Ops:
  0.0 79.3 %shard_map.46 = f32[6,16,8,16]{3,2,1,0:T(8,128)} custom-call(bf16[6,16,16,96]{3,2,1,0:T(8,128)(2,1)} %val_ref.1, bf16[6,16,8,96]{3,2,1,0:T(8,128)(2,1)} %con_ref.1, bf16[1,96,4608]{2,1,0:T(8,128)(2,1)} %w_hbm.1, s32[6,16]{1,0:T(8,128)} %table_hbm.1), custom_call_target="tpu_custom_call" | custom-call | tf_op jit(solution)/shard_map/pallas_call | solution.py:269
  79.3 1.8 %copy.6 = f32[6,16,8,16]{3,2,1,0:T(8,128)} copy(f32[6,16,8,16]{3,2,1,0:T(8,128)} %shard_map.46) | data formatting | bytes 98304
